TPU v7x, 32 devices: a whole 2x2x4 slice. The times are simulated.
32 devices in a mesh: dp: 8 (over z, y), expert: 4 (over x, core).
Axes of the slice: x: 2, y: 2, z: 4, core: 2. Of those that a mesh axis runs over, the one named last changes fastest.
Arguments:
- master_old: float32 [8, 4, 16, 128], P('dp', 'expert'), may hold values from -1.5 to 1.5
- m_codes: bfloat16 [8, 4, 16, 128], P('dp', 'expert'), may hold values from -1 to 1
- m_scale: float32 [8, 4, 16], P('dp', 'expert'), may hold values from 0.05 to 0.5
- v_codes: bfloat16 [8, 4, 16, 128], P('dp', 'expert'), may hold values from 0.049804688 to 1
- v_scale: float32 [8, 4, 16], P('dp', 'expert'), may hold values from 0.1 to 1
- grad_parts: bfloat16 [8, 4, 128, 128], P('dp', 'expert'), may hold values from -100 to 100, as said below
- send_order: int32 [8, 4, 16], P('dp', 'expert'), may hold values from 0 to 15, each once within a row
- recv_place: int32 [8, 4, 16], P('dp', 'expert'), may hold values from 0 to 15, each once within a row
Outputs:
- master_new: float32 [4, 128, 128], P('expert', 'dp')
- m_codes_new: bfloat16 [4, 128, 128], P('expert', 'dp')
- m_scale_new: float32 [4, 128], P('expert', 'dp')
- v_codes_new: bfloat16 [4, 128, 128], P('expert', 'dp')
- v_scale_new: float32 [4, 128], P('expert', 'dp')
Inputs may be any that keep to these rules, and one draw needn't show every extreme that they name: `grad_parts`: partial gradients of one data shard.
All inputs are finite; a program needn't handle non-finite values. Where the computation divides by a largest or mean magnitude, that divisor is 1e-20 or more.
Results may differ from a plain program's by a relative error of at most 0.0004.
Values may be sent and summed in bfloat16 or wider, within the bound.
A program may use at most 64 MiB of HBM per device.

v0:
```python
import jax
import jax.numpy as jnp
from jax import lax
from jax.sharding import PartitionSpec as P

STEP = 200


BETA_ONE = 0.9
BETA_TWO = 0.999
ADAM_EPS = 1e-08
LEARN_RATE = 0.05
DECAY_RATE = 0.1
CLIP_RMS = 1.0
QUANT_EPS = 1e-06
NORM_EPS = 1e-06


def dequant(codes, scales):
    return codes.astype(jnp.float32) * scales[..., None]


def requant(moment):
    magnitude = jnp.max(jnp.abs(moment), axis=-1) + QUANT_EPS
    return ((moment / magnitude[..., None]).astype(jnp.bfloat16), magnitude)


def body(master_old, m_codes, m_scale, v_codes, v_scale, grad_parts, send_order, recv_place):
    order_rows = send_order[0, 0]
    inverse = jnp.argsort(recv_place[0, 0])
    summed = lax.psum_scatter(grad_parts.astype(jnp.float32), "dp", scatter_dimension=2, tiled=True)
    gradient = summed[0]
    local_squares = jnp.sum(gradient * gradient)
    total_squares = lax.psum(local_squares, ("dp", "expert"))
    entry_count = (
        lax.axis_size("dp") * lax.axis_size("expert") * gradient.shape[1] * gradient.shape[2]
    )
    root_mean = jnp.sqrt(total_squares / entry_count + NORM_EPS)
    clip_factor = jnp.minimum(1.0, CLIP_RMS / root_mean)
    arrived = (
        lax.all_to_all(
            jnp.take(master_old, order_rows, axis=2),
            "expert",
            split_axis=2,
            concat_axis=2,
            tiled=True,
        ),
        lax.all_to_all(
            jnp.take(dequant(m_codes, m_scale), order_rows, axis=2),
            "expert",
            split_axis=2,
            concat_axis=2,
            tiled=True,
        ),
        lax.all_to_all(
            jnp.take(dequant(v_codes, v_scale), order_rows, axis=2),
            "expert",
            split_axis=2,
            concat_axis=2,
            tiled=True,
        ),
    )
    placed = [jnp.take(member, inverse, axis=2)[0] for member in arrived]
    master = placed[0]
    moment_one = placed[1]
    moment_two = placed[2]
    clipped = clip_factor * gradient
    m_next = BETA_ONE * moment_one + (1.0 - BETA_ONE) * clipped
    v_next = BETA_TWO * moment_two + (1.0 - BETA_TWO) * clipped * clipped
    bias_one = 1.0 - BETA_ONE**STEP
    bias_two = 1.0 - BETA_TWO**STEP
    update = m_next / bias_one / (jnp.sqrt(v_next / bias_two) + ADAM_EPS)
    master_new = master - LEARN_RATE * (update + DECAY_RATE * master)
    m_codes_new, m_scale_new = requant(m_next)
    v_codes_new, v_scale_new = requant(v_next)
    return (master_new, m_codes_new, m_scale_new, v_codes_new, v_scale_new)


def solution(mesh):
    placed = (
        P("dp", "expert", None, None),
        P("dp", "expert", None, None),
        P("dp", "expert", None),
        P("dp", "expert", None, None),
        P("dp", "expert", None),
        P("dp", "expert", None, None),
        P("dp", "expert", None),
        P("dp", "expert", None),
    )
    return jax.shard_map(
        body,
        mesh=mesh,
        in_specs=placed,
        out_specs=(
            P("expert", "dp", None),
            P("expert", "dp", None),
            P("expert", "dp"),
            P("expert", "dp", None),
            P("expert", "dp"),
        ),
        check_vma=False,
    )
```

profile of v0, /device:TPU:0, one launch (start us, length us, event | category | flops | bytes accessed | tf_op | source)
XLA Modules:
  0.0 126.5 jit_solution(8882549962534562566)
XLA Ops:
  7.2 0.0 copy-start
  7.2 0.0 reduce-scatter.2.cloned.1.call-start
  7.2 1.4 %convert_element_type.32 = f32[1,1,128,128]{3,2,1,0:T(8,128)} convert(bf16[1,1,128,128]{3,2,1,0:T(8,128)(2,1)} %param.15) | non-fusion elementwise | flops 16384 | bytes 98304 | tf_op jit(solution)/shard_map/convert_element_type | solution.py:31
  8.6 0.0 copy-start.6
  8.6 0.0 reduce-scatter.2.cloned.1.call-update
  8.6 0.6 copy-done.6
  9.3 0.0 copy-start.2
  9.3 0.0 copy-start.4
  9.3 0.7 copy-done.2
  10.0 0.0 copy-done.4
  10.0 0.1 multiply_bitcast_fusion
  10.0 0.0 copy-start.3
  10.0 0.6 gather_fusion.4
  10.6 0.0 copy-start.5
  10.6 0.1 copy-done.3
  10.7 0.5 copy-done.5
  11.3 0.1 multiply_bitcast_fusion.1
  11.3 0.6 gather_fusion.2
  11.9 0.0 copy-done
  11.9 0.6 gather_fusion
  12.5 0.7 bitcast_select_fusion.1
  13.1 4.2 %all-to-all-start.2 = ((f32[1,1,16,128]{3,1,0,2:T(1,128)}), f32[1,1,16,128]{3,1,0,2:T(1,128)S(1)}, u32[]{:S(2)}, u32[]{:S(2)}) async-start(f32[1,1,16,128]{3,1,0,2:T(1,128)} %bitcast.19), calls=%async_computation.3 | async-start | bytes 16384 | tf_op jit(solution)/shard_map/all_to_all | solution.py:55
  17.3 0.0 copy-start.7
  17.4 0.7 copy-done.7
  18.0 1.2 sort.17
  19.3 1.9 %all-to-all-done.2 = f32[1,1,16,128]{3,1,0,2:T(1,128)S(1)} async-done(((f32[1,1,16,128]{3,1,0,2:T(1,128)}), f32[1,1,16,128]{3,1,0,2:T(1,128)S(1)}, u32[]{:S(2)}, u32[]{:S(2)}) %all-to-all-start.2) | async-done | bytes 8224 | tf_op jit(solution)/shard_map/all_to_all | solution.py:55
  21.2 3.2 %all-to-all-start.1 = ((f32[1,1,16,128]{3,1,0,2:T(1,128)}), f32[1,1,16,128]{3,1,0,2:T(1,128)S(1)}, u32[]{:S(2)}, u32[]{:S(2)}) async-start(f32[1,1,16,128]{3,1,0,2:T(1,128)} %bitcast.11), calls=%async_computation.1 | async-start | bytes 16384 | tf_op jit(solution)/shard_map/all_to_all | solution.py:48
  24.4 0.6 gather_fusion.5
  25.0 3.2 %all-to-all-done.1 = f32[1,1,16,128]{3,1,0,2:T(1,128)S(1)} async-done(((f32[1,1,16,128]{3,1,0,2:T(1,128)}), f32[1,1,16,128]{3,1,0,2:T(1,128)S(1)}, u32[]{:S(2)}, u32[]{:S(2)}) %all-to-all-start.1) | async-done | bytes 8224 | tf_op jit(solution)/shard_map/all_to_all | solution.py:48
  28.2 3.2 %all-to-all-start = ((f32[1,1,16,128]{3,1,0,2:T(1,128)}), f32[1,1,16,128]{3,1,0,2:T(1,128)S(1)}, u32[]{:S(2)}, u32[]{:S(2)}) async-start(f32[1,1,16,128]{3,1,0,2:T(1,128)} %bitcast.4), calls=%async_computation | async-start | bytes 16384 | tf_op jit(solution)/shard_map/all_to_all | solution.py:41
  31.4 0.6 gather_fusion.3
  32.0 43.3 %reduce-scatter.2.cloned.1.call-done = f32[1,1,16,128]{3,2,1,0:T(8,128)} async-done(((f32[1,1,128,128]{3,2,1,0:T(8,128)}), f32[1,1,16,128]{3,2,1,0:T(8,128)}) %reduce-scatter.2.cloned.1.call-update) | async-done | bytes 8208 | tf_op jit(solution)/shard_map/reduce_scatter | solution.py:31
  75.4 1.3 %multiply_reduce_fusion = f32[]{:T(128)} fusion(f32[1,1,16,128]{3,2,1,0:T(8,128)} %reduce-scatter.2.cloned.1.call-done), kind=kLoop, calls=%fused_computation.27 | loop fusion | flops 4095 | bytes 8196 | tf_op jit(solution)/shard_map/reduce_sum | solution.py:33
  76.7 0.0 all-to-all-done
  76.7 0.6 gather_fusion.1
  77.2 0.0 copy-start.1
  77.2 40.3 %psum.7 = f32[]{:T(128)} all-reduce(f32[]{:T(128)} %multiply_reduce_fusion), channel_id=1, replica_groups=mesh['dp'=8,'expert'=4] {'dp','expert'}, use_global_device_ids=true, to_apply=%region_3.0 | all-reduce | flops 1 | bytes 8 | tf_op jit(solution)/shard_map/psum | solution.py:34
  118.2 0.0 copy-done.1
  118.3 0.2 abs_reduce_fusion
  118.4 0.5 fusion.6
  119.0 0.7 divide_convert_fusion
  (7 shorter events, 0.0 us)
Async XLA Ops:
  7.2 4.7 %copy-start = (f32[1,1,16,128]{3,2,1,0:T(8,128)S(1)}, f32[1,1,16,128]{3,2,1,0:T(8,128)}, u32[]{:S(2)}) copy-start(f32[1,1,16,128]{3,2,1,0:T(8,128)} %param.10) | copy-start | bytes 24580
  7.2 68.2 %reduce-scatter.2.cloned.1.call-start = ((), (), s32[]{:S(2)}) async-start(), calls=%async_computation.4 | async-start | bytes 73728 | tf_op jit(solution)/shard_map/reduce_scatter | solution.py:31
  8.6 0.7 copy-start.6
  9.3 0.7 copy-start.2
  9.3 0.7 copy-start.4
  10.0 0.7 copy-start.3
  10.6 0.7 copy-start.5
  13.1 8.0 %all-to-all-start.2 = ((f32[1,1,16,128]{3,1,0,2:T(1,128)}), f32[1,1,16,128]{3,1,0,2:T(1,128)S(1)}, u32[]{:S(2)}, u32[]{:S(2)}) async-start(f32[1,1,16,128]{3,1,0,2:T(1,128)} %bitcast.19), calls=%async_computation.3 | async-start | bytes 16384 | tf_op jit(solution)/shard_map/all_to_all | solution.py:55
  17.3 0.7 copy-start.7
  21.2 7.0 %all-to-all-start.1 = ((f32[1,1,16,128]{3,1,0,2:T(1,128)}), f32[1,1,16,128]{3,1,0,2:T(1,128)S(1)}, u32[]{:S(2)}, u32[]{:S(2)}) async-start(f32[1,1,16,128]{3,1,0,2:T(1,128)} %bitcast.11), calls=%async_computation.1 | async-start | bytes 16384 | tf_op jit(solution)/shard_map/all_to_all | solution.py:48
  28.2 48.5 %all-to-all-start = ((f32[1,1,16,128]{3,1,0,2:T(1,128)}), f32[1,1,16,128]{3,1,0,2:T(1,128)S(1)}, u32[]{:S(2)}, u32[]{:S(2)}) async-start(f32[1,1,16,128]{3,1,0,2:T(1,128)} %bitcast.4), calls=%async_computation | async-start | bytes 16384 | tf_op jit(solution)/shard_map/all_to_all | solution.py:41
  77.2 41.0 %copy-start.1 = (f32[1,1,16,128]{3,2,1,0:T(8,128)S(1)}, f32[1,1,16,128]{3,2,1,0:T(8,128)}, u32[]{:S(2)}) copy-start(f32[1,1,16,128]{3,2,1,0:T(8,128)} %reduce-scatter.2.cloned.1.call-done) | copy-start | bytes 24580
Sparse Core Ops, SparseCore 0:
  11.4 63.8 reduce-scatter.1
where the time goes:
time: 127 us; the launch traced here: 126 us
  waiting for transfers between devices  48.5 us (38%)
  blocking collectives  40.3 us (32%)
  between operations  14.8 us (12%)
  starting transfers between devices  10.7 us (8%)
  other arithmetic  6.17 us (5%)
  local copies, waits for them, and re-layouts  5.98 us (5%)
    reduce_scatter x1, waiting for transfers between devices, body(): lax.psum_scatter(grad_parts.astype(jnp.float32), 'dp', scatter_dimension=...  43.3 us
    psum x1, blocking collectives, body(): total_squares = lax.psum(local_squares, ('dp', 'expert'))  40.3 us
    all_to_all x1, starting transfers between devices, body(): lax.all_to_all(jnp.take(dequant(v_codes, v_scale), order_rows, axis=2), '...  4.21 us
    all_to_all x1, starting transfers between devices, body(): lax.all_to_all(jnp.take(dequant(m_codes, m_scale), order_rows, axis=2), '...  3.25 us
    all_to_all x1, starting transfers between devices, body(): lax.all_to_all(jnp.take(master_old, order_rows, axis=2), 'expert', split_...  3.23 us
    all_to_all x1, waiting for transfers between devices, body(): lax.all_to_all(jnp.take(dequant(m_codes, m_scale), order_rows, axis=2), '...  3.2 us
    unnamed x16, local copies, waits for them, and re-layouts  2.61 us
  transfers between devices with their start and end apart: 4, of which 3 were waited for; matrix products, arithmetic and copies ran while one was open for 5% of the time, Pallas kernels for 0%

commit v1 on v0

v1 whole, which is shorter than its diff:
```python
import functools

import jax
import jax.numpy as jnp
from jax import lax
from jax.experimental import pallas as pl
from jax.experimental.pallas import tpu as pltpu
from jax.sharding import PartitionSpec as P

STEP = 200

BETA_ONE = 0.9
BETA_TWO = 0.999
ADAM_EPS = 1e-08
LEARN_RATE = 0.05
DECAY_RATE = 0.1
CLIP_RMS = 1.0
QUANT_EPS = 1e-06
NORM_EPS = 1e-06

MESH = pl.DeviceIdType.MESH
UNROLL = 40


def each(first, last, step):
    if last - first <= UNROLL:
        for k in range(first, last):
            step(k)
    else:
        lax.fori_loop(first, last, lambda k, c: (step(k), c)[1], 0)


def kernel(
    shards, groups,
    master_in, mc_in, ms_in, vc_in, vs_in, grads_in, order_in, place_in,
    master_out, mc_out, ms_out, vc_out, vs_out,
    master_v, mc_v, vc_v, grads_v, m_wide, v_wide,
    ms_s, vs_s, order_s, place_s,
    relay_out, relay_in, grad_in, square_out, square_in,
    in_sems, grad_sems, relay_sems, square_sems,
):
    d = lax.axis_index("dp")
    e = lax.axis_index("expert")
    blocks, block = master_v.shape
    q = blocks // groups
    total = shards * groups

    barrier = pltpu.get_barrier_semaphore()

    def greet_shard(k):
        pl.semaphore_signal(barrier, inc=1, device_id=(lax.rem(d + k, shards), e), device_id_type=MESH)

    def greet_group(k):
        pl.semaphore_signal(barrier, inc=1, device_id=(d, lax.rem(e + k, groups)), device_id_type=MESH)

    each(1, shards, greet_shard)
    each(1, groups, greet_group)

    loads = [
        pltpu.make_async_copy(src, dst, in_sems.at[i])
        for i, (src, dst) in enumerate((
            (grads_in, grads_v), (order_in, order_s), (ms_in, ms_s), (vs_in, vs_s),
            (mc_in, mc_v), (vc_in, vc_v), (master_in, master_v), (place_in, place_s),
        ))
    ]
    for load in loads:
        load.start()
    loads[0].wait()
    pl.semaphore_wait(barrier, shards - 1 + groups - 1)

    def grad_copy(k):
        to = lax.rem(d + k, shards)
        return pltpu.make_async_remote_copy(
            src_ref=grads_v.at[to], dst_ref=grad_in.at[k - 1],
            send_sem=grad_sems.at[0], recv_sem=grad_sems.at[1],
            device_id=(to, e), device_id_type=MESH)

    each(1, shards, lambda k: grad_copy(k).start())

    for load in loads[1:]:
        load.wait()
    m_wide[...] = mc_v[...].astype(jnp.float32)
    v_wide[...] = vc_v[...].astype(jnp.float32)

    def relay_copy(k):
        to = lax.rem(e + k, groups)
        return pltpu.make_async_remote_copy(
            src_ref=relay_out.at[k], dst_ref=relay_in.at[k - 1],
            send_sem=relay_sems.at[0], recv_sem=relay_sems.at[1],
            device_id=(d, to), device_id_type=MESH)

    for k in list(range(1, groups)) + [0]:
        to = lax.rem(e + k, groups)
        for c in range(q):
            row = order_s[0, to * q + c]
            relay_out[k, 0, c : c + 1, :] = master_v[pl.ds(row, 1), :]
            relay_out[k, 1, c : c + 1, :] = m_wide[pl.ds(row, 1), :] * ms_s[0, row]
            relay_out[k, 2, c : c + 1, :] = v_wide[pl.ds(row, 1), :] * vs_s[0, row]
        if k:
            relay_copy(k).start()

    whole = pltpu.make_async_remote_copy(
        src_ref=grad_in, dst_ref=grad_in, send_sem=grad_sems.at[0], recv_sem=grad_sems.at[1],
        device_id=(lax.rem(d + 1, shards), e), device_id_type=MESH)
    whole.wait_recv()
    gradient = grads_v[d].astype(jnp.float32)
    if shards - 1 <= UNROLL:
        for k in range(shards - 1):
            gradient = gradient + grad_in[k].astype(jnp.float32)
    else:
        gradient = lax.fori_loop(
            0, shards - 1, lambda k, g: g + grad_in[k].astype(jnp.float32), gradient)
    squares = jnp.sum(gradient * gradient, axis=0, keepdims=True)
    square_out[...] = squares

    def square_copy(k):
        flat = lax.rem(d * groups + e + k, total)
        return pltpu.make_async_remote_copy(
            src_ref=square_out, dst_ref=square_in.at[k - 1],
            send_sem=square_sems.at[0], recv_sem=square_sems.at[1],
            device_id=(flat // groups, lax.rem(flat, groups)), device_id_type=MESH)

    each(1, total, lambda k: square_copy(k).start())

    relay_whole = pltpu.make_async_remote_copy(
        src_ref=relay_in, dst_ref=relay_in, send_sem=relay_sems.at[0], recv_sem=relay_sems.at[1],
        device_id=(d, lax.rem(e + 1, groups)), device_id_type=MESH)
    relay_whole.wait_recv()
    rows = lax.broadcasted_iota(jnp.int32, (blocks, block), 0)
    placed = [jnp.zeros((blocks, block), jnp.float32) for _ in range(3)]
    for k in range(groups):
        frm = lax.rem(e - k + groups, groups)
        for c in range(q):
            here = rows == place_s[0, frm * q + c]
            for i in range(3):
                row = relay_out[0, i, c : c + 1, :] if k == 0 else relay_in[k - 1, i, c : c + 1, :]
                placed[i] = jnp.where(here, jnp.broadcast_to(row, (blocks, block)), placed[i])
    master, moment_one, moment_two = placed

    square_whole = pltpu.make_async_remote_copy(
        src_ref=square_in, dst_ref=square_in, send_sem=square_sems.at[0], recv_sem=square_sems.at[1],
        device_id=(lax.rem(d + 1, shards), e), device_id_type=MESH)
    square_whole.wait_recv()
    lanes = jnp.sum(square_in[...], axis=0) + squares
    total_squares = jnp.sum(lanes, axis=1, keepdims=True)
    root_mean = jnp.sqrt(total_squares / (total * blocks * block) + NORM_EPS)
    clip_factor = jnp.minimum(1.0, CLIP_RMS / root_mean)

    clipped = clip_factor * gradient
    m_next = BETA_ONE * moment_one + (1.0 - BETA_ONE) * clipped
    v_next = BETA_TWO * moment_two + (1.0 - BETA_TWO) * clipped * clipped
    bias_one = 1.0 - BETA_ONE**STEP
    bias_two = 1.0 - BETA_TWO**STEP
    m_mag = jnp.max(jnp.abs(m_next), axis=1, keepdims=True) + QUANT_EPS
    v_mag = jnp.max(jnp.abs(v_next), axis=1, keepdims=True) + QUANT_EPS
    update = m_next / bias_one / (jnp.sqrt(v_next / bias_two) + ADAM_EPS)
    master_out[...] = master - LEARN_RATE * (update + DECAY_RATE * master)
    mc_out[...] = (m_next / m_mag).astype(jnp.bfloat16)
    vc_out[...] = (v_next / v_mag).astype(jnp.bfloat16)
    diagonal = rows == lax.broadcasted_iota(jnp.int32, (blocks, block), 1)
    ms_out[...] = jnp.sum(jnp.where(diagonal, m_mag, 0.0), axis=0, keepdims=True)[:, :blocks]
    vs_out[...] = jnp.sum(jnp.where(diagonal, v_mag, 0.0), axis=0, keepdims=True)[:, :blocks]

    whole.wait_send()
    relay_whole.wait_send()
    square_whole.wait_send()


def body(shards, groups, master_old, m_codes, m_scale, v_codes, v_scale, grad_parts, send_order, recv_place):
    blocks, block = master_old.shape[2:]
    q = blocks // groups
    f32, bf16 = jnp.float32, jnp.bfloat16
    wide = (blocks, block)
    anywhere = pl.BlockSpec(memory_space=pl.ANY)
    vmem = pl.BlockSpec(memory_space=pltpu.VMEM)
    master_new, mc, ms, vc, vs = pl.pallas_call(
        functools.partial(kernel, shards, groups),
        out_shape=(
            jax.ShapeDtypeStruct(wide, f32),
            jax.ShapeDtypeStruct(wide, bf16),
            jax.ShapeDtypeStruct((1, blocks), f32),
            jax.ShapeDtypeStruct(wide, bf16),
            jax.ShapeDtypeStruct((1, blocks), f32),
        ),
        in_specs=[anywhere] * 8,
        out_specs=(vmem,) * 5,
        scratch_shapes=[
            pltpu.VMEM(wide, f32),
            pltpu.VMEM(wide, bf16),
            pltpu.VMEM(wide, bf16),
            pltpu.VMEM((shards, blocks, block), bf16),
            pltpu.VMEM(wide, f32),
            pltpu.VMEM(wide, f32),
            pltpu.SMEM((1, blocks), f32),
            pltpu.SMEM((1, blocks), f32),
            pltpu.SMEM((1, blocks), jnp.int32),
            pltpu.SMEM((1, blocks), jnp.int32),
            pltpu.VMEM((groups, 3, q, block), f32),
            pltpu.VMEM((groups - 1, 3, q, block), f32),
            pltpu.VMEM((shards - 1, blocks, block), bf16),
            pltpu.VMEM((1, block), f32),
            pltpu.VMEM((shards * groups - 1, 1, block), f32),
            pltpu.SemaphoreType.DMA((8,)),
            pltpu.SemaphoreType.DMA((2,)),
            pltpu.SemaphoreType.DMA((2,)),
            pltpu.SemaphoreType.DMA((2,)),
        ],
        compiler_params=pltpu.CompilerParams(collective_id=0, has_side_effects=True),
    )(
        master_old.reshape(wide), m_codes.reshape(wide), m_scale.reshape(1, blocks),
        v_codes.reshape(wide), v_scale.reshape(1, blocks),
        grad_parts.reshape(shards, blocks, block),
        send_order.reshape(1, blocks), recv_place.reshape(1, blocks),
    )
    return master_new[None], mc[None], ms, vc[None], vs


def solution(mesh):
    rows = P("dp", "expert", None, None)
    flat = P("dp", "expert", None)
    return jax.shard_map(
        functools.partial(body, mesh.shape["dp"], mesh.shape["expert"]),
        mesh=mesh,
        in_specs=(rows, rows, flat, rows, flat, rows, flat, flat),
        out_specs=(
            P("expert", "dp", None),
            P("expert", "dp", None),
            P("expert", "dp"),
            P("expert", "dp", None),
            P("expert", "dp"),
        ),
        check_vma=False,
    )
```

time: 127 us -> 20.6 us (0.16)
  waiting for transfers between devices: 48.5 us -> 0 us
  blocking collectives: 40.3 us -> 0 us
  Pallas kernels: 0 us -> 16 us
  between operations: 14.8 us -> 0.66 us
  starting transfers between devices: 10.7 us -> 0 us
  other arithmetic: 6.17 us -> 0 us
  local copies, waits for them, and re-layouts: 5.98 us -> 3.71 us
    reduce_scatter x1 -> x0, waiting for transfers between devices: 43.3 us -> none  [body(): lax.psum_scatter(grad_parts.astype(jnp.float32), 'dp', scatter_dimension=...]
    psum x1 -> x0, blocking collectives: 40.3 us -> none  [body(): total_squares = lax.psum(local_squares, ('dp', 'expert'))]
    pallas_call x0 -> x1, Pallas kernels: none -> 16 us  [body(): pl.pallas_call(functools.partial(kernel, shards, groups), out_shape=(jax....]
    all_to_all x3 -> x0, starting transfers between devices: 10.7 us -> none  [the longest x1 4.21 us: body(): lax.all_to_all(jnp.take(dequant(v_codes, v_scale), order_rows, axis=2), '...]
    all_to_all x3 -> x0, waiting for transfers between devices: 5.11 us -> none  [the longest x1 3.2 us: body(): lax.all_to_all(jnp.take(dequant(m_codes, m_scale), order_rows, axis=2), '...]
    gather x6 -> x0, local copies, waits for them, and re-layouts: 3.37 us -> none  [the longest x3 1.68 us: body(): placed = [jnp.take(member, inverse, axis=2)[0] for member in arrived]]
    convert_element_type x2 -> x0, other arithmetic: 2.06 us -> none  [the longest x1 1.38 us: body(): grad_parts.astype(jnp.float32)]
    reduce_sum x1 -> x0, other arithmetic: 1.3 us -> none  [body(): local_squares = jnp.sum(gradient * gradient)]
  transfers between devices with their start and end apart: 4 -> 0, of which waited for: 3 -> 0; matrix products, arithmetic and copies ran while one was open for 5% -> 0% of each run, Pallas kernels for 0% -> 0%
where the time goes in v1:
time: 20.6 us; the launch traced here: 20.3 us
  Pallas kernels  16 us (78%)
  local copies, waits for them, and re-layouts  3.71 us (18%)
  between operations  0.66 us (3%)
    pallas_call x1, Pallas kernels, body(): pl.pallas_call(functools.partial(kernel, shards, groups), out_shape=(jax....  16 us
    unnamed x15, local copies, waits for them, and re-layouts  3.71 us

profile of v1, /device:TPU:0, one launch (start us, length us, event | category | flops | bytes accessed | tf_op | source)
XLA Modules:
  0.0 20.3 jit_solution(15843272261862551228)
XLA Ops:
  0.6 16.0 %shard_map.119 = (f32[16,128]{1,0:T(8,128)}, bf16[16,128]{1,0:T(8,128)(2,1)}, f32[1,16]{1,0:T(1,128)}, bf16[16,128]{1,0:T(8,128)(2,1)}, f32[1,16]{1,0:T(1,128)}) custom-call(f32[16,128]{1,0:T(8,128)} %bitcast.12, bf16[16,128]{1,0:T(8,128)(2,1)} %bitcast.14, f32[1,16]{1,0:T(1,128)} %bitcast.18, bf16[16,128]{1,0:T(8,128)(2,1)} %bitcast.15, f32[1,16]{1,0:T(1,128)} %bitcast.19, ...), custom_call_target="tpu_custom_call" | custom-call | tf_op jit(solution)/shard_map/pallas_call | solution.py:176
  16.6 0.0 copy-start
  16.6 0.7 %copy-done = f32[16,128]{1,0:T(8,128)S(1)} copy-done((f32[16,128]{1,0:T(8,128)S(1)}, f32[16,128]{1,0:T(8,128)}, u32[]{:S(2)}) %copy-start) | copy-done | bytes 8216
  17.3 0.0 copy-start.2
  17.3 0.6 %copy.18 = f32[1,16,128]{2,1,0:T(8,128)} copy(f32[1,16,128]{2,1,0:T(8,128)S(1)} %bitcast.13) | data formatting | bytes 16384
  17.9 0.1 copy-done.2
  18.0 0.0 copy-start.4
  18.0 0.0 copy-start.1
  18.0 0.6 %copy.19 = bf16[1,16,128]{2,1,0:T(8,128)(2,1)} copy(bf16[1,16,128]{2,1,0:T(8,128)(2,1)S(1)} %bitcast.17) | data formatting | bytes 8192
  18.6 0.1 copy-done.4
  18.7 0.5 %copy.20 = f32[1,16]{1,0:T(1,128)} copy(f32[1,16]{1,0:T(1,128)S(1)} %copy-done.4) | data formatting | bytes 128
  19.2 0.0 copy-done.1
  19.2 0.0 copy-start.3
  19.2 0.6 %copy.21 = bf16[1,16,128]{2,1,0:T(8,128)(2,1)} copy(bf16[1,16,128]{2,1,0:T(8,128)(2,1)S(1)} %bitcast.16) | data formatting | bytes 8192
  19.8 0.1 copy-done.3
  19.8 0.5 %copy.22 = f32[1,16]{1,0:T(1,128)} copy(f32[1,16]{1,0:T(1,128)S(1)} %copy-done.3) | data formatting | bytes 128
Async XLA Ops:
  16.6 0.7 %copy-start = (f32[16,128]{1,0:T(8,128)S(1)}, f32[16,128]{1,0:T(8,128)}, u32[]{:S(2)}) copy-start(f32[16,128]{1,0:T(8,128)} %get-tuple-element.10) | copy-start | bytes 24580
  17.3 0.7 %copy-start.2 = (bf16[16,128]{1,0:T(8,128)(2,1)S(1)}, bf16[16,128]{1,0:T(8,128)(2,1)}, u32[]{:S(2)}) copy-start(bf16[16,128]{1,0:T(8,128)(2,1)} %get-tuple-element.11) | copy-start | bytes 12292
  18.0 0.7 %copy-start.4 = (f32[1,16]{1,0:T(1,128)S(1)}, f32[1,16]{1,0:T(1,128)}, u32[]{:S(2)}) copy-start(f32[1,16]{1,0:T(1,128)} %get-tuple-element.22) | copy-start | bytes 196
  18.0 1.2 %copy-start.1 = (bf16[16,128]{1,0:T(8,128)(2,1)S(1)}, bf16[16,128]{1,0:T(8,128)(2,1)}, u32[]{:S(2)}) copy-start(bf16[16,128]{1,0:T(8,128)(2,1)} %get-tuple-element.13) | copy-start | bytes 12292
  19.2 0.7 %copy-start.3 = (f32[1,16]{1,0:T(1,128)S(1)}, f32[1,16]{1,0:T(1,128)}, u32[]{:S(2)}) copy-start(f32[1,16]{1,0:T(1,128)} %get-tuple-element.24) | copy-start | bytes 196

commit v2 on v1

--- a/solution.py
+++ b/solution.py
@@ -33,7 +33,7 @@
 def kernel(
     shards, groups,
     master_in, mc_in, ms_in, vc_in, vs_in, grads_in, order_in, place_in,
-    master_out, mc_out, ms_out, vc_out, vs_out,
+    state_out, lanes_out,
     master_v, mc_v, vc_v, grads_v, m_wide, v_wide,
     ms_s, vs_s, order_s, place_s,
     relay_out, relay_in, grad_in, square_out, square_in,
@@ -137,13 +137,27 @@
                 placed[i] = jnp.where(here, jnp.broadcast_to(row, (blocks, block)), placed[i])
     master, moment_one, moment_two = placed
 
+    for i in range(3):
+        state_out[i + 1] = placed[i]
+    state_out[0] = gradient
+
     square_whole = pltpu.make_async_remote_copy(
         src_ref=square_in, dst_ref=square_in, send_sem=square_sems.at[0], recv_sem=square_sems.at[1],
         device_id=(lax.rem(d + 1, shards), e), device_id_type=MESH)
     square_whole.wait_recv()
-    lanes = jnp.sum(square_in[...], axis=0) + squares
-    total_squares = jnp.sum(lanes, axis=1, keepdims=True)
-    root_mean = jnp.sqrt(total_squares / (total * blocks * block) + NORM_EPS)
+    lanes_out[...] = jnp.sum(square_in[...], axis=0) + squares
+
+    whole.wait_send()
+    relay_whole.wait_send()
+    square_whole.wait_send()
+
+
+def update(count, state, lanes, master_out, mc_out, ms_out, vc_out, vs_out):
+    gradient, master, moment_one, moment_two = (state[i] for i in range(4))
+    blocks, block = gradient.shape
+
+    total_squares = jnp.sum(lanes[...], axis=1, keepdims=True)
+    root_mean = jnp.sqrt(total_squares / count + NORM_EPS)
     clip_factor = jnp.minimum(1.0, CLIP_RMS / root_mean)
 
     clipped = clip_factor * gradient
@@ -153,17 +167,14 @@
     bias_two = 1.0 - BETA_TWO**STEP
     m_mag = jnp.max(jnp.abs(m_next), axis=1, keepdims=True) + QUANT_EPS
     v_mag = jnp.max(jnp.abs(v_next), axis=1, keepdims=True) + QUANT_EPS
-    update = m_next / bias_one / (jnp.sqrt(v_next / bias_two) + ADAM_EPS)
-    master_out[...] = master - LEARN_RATE * (update + DECAY_RATE * master)
+    step = m_next / bias_one / (jnp.sqrt(v_next / bias_two) + ADAM_EPS)
+    master_out[...] = master - LEARN_RATE * (step + DECAY_RATE * master)
     mc_out[...] = (m_next / m_mag).astype(jnp.bfloat16)
     vc_out[...] = (v_next / v_mag).astype(jnp.bfloat16)
+    rows = lax.broadcasted_iota(jnp.int32, (blocks, block), 0)
     diagonal = rows == lax.broadcasted_iota(jnp.int32, (blocks, block), 1)
     ms_out[...] = jnp.sum(jnp.where(diagonal, m_mag, 0.0), axis=0, keepdims=True)[:, :blocks]
     vs_out[...] = jnp.sum(jnp.where(diagonal, v_mag, 0.0), axis=0, keepdims=True)[:, :blocks]
-
-    whole.wait_send()
-    relay_whole.wait_send()
-    square_whole.wait_send()
 
 
 def body(shards, groups, master_old, m_codes, m_scale, v_codes, v_scale, grad_parts, send_order, recv_place):
@@ -173,17 +184,11 @@
     wide = (blocks, block)
     anywhere = pl.BlockSpec(memory_space=pl.ANY)
     vmem = pl.BlockSpec(memory_space=pltpu.VMEM)
-    master_new, mc, ms, vc, vs = pl.pallas_call(
+    state, lanes = pl.pallas_call(
         functools.partial(kernel, shards, groups),
-        out_shape=(
-            jax.ShapeDtypeStruct(wide, f32),
-            jax.ShapeDtypeStruct(wide, bf16),
-            jax.ShapeDtypeStruct((1, blocks), f32),
-            jax.ShapeDtypeStruct(wide, bf16),
-            jax.ShapeDtypeStruct((1, blocks), f32),
-        ),
+        out_shape=(pltpu.VMEM((4, blocks, block), f32), pltpu.VMEM((1, block), f32)),
         in_specs=[anywhere] * 8,
-        out_specs=(vmem,) * 5,
+        out_specs=(vmem, vmem),
         scratch_shapes=[
             pltpu.VMEM(wide, f32),
             pltpu.VMEM(wide, bf16),
@@ -212,6 +217,20 @@
         grad_parts.reshape(shards, blocks, block),
         send_order.reshape(1, blocks), recv_place.reshape(1, blocks),
     )
+    master_new, mc, ms, vc, vs = pl.pallas_call(
+        functools.partial(update, shards * groups * blocks * block),
+        out_shape=(
+            jax.ShapeDtypeStruct(wide, f32),
+            jax.ShapeDtypeStruct(wide, bf16),
+            jax.ShapeDtypeStruct((1, blocks), f32),
+            jax.ShapeDtypeStruct(wide, bf16),
+            jax.ShapeDtypeStruct((1, blocks), f32),
+        ),
+        in_specs=[vmem, vmem],
+        out_specs=(vmem,) * 5,
+    )(
+        pltpu.with_memory_space_constraint(state, pltpu.VMEM),
+        pltpu.with_memory_space_constraint(lanes, pltpu.VMEM))
     return master_new[None], mc[None], ms, vc[None], vs
 
 

time: 20.6 us -> 16.8 us (0.82)
  local copies, waits for them, and re-layouts: 3.71 us -> 0 us
    unnamed x15 -> x0, local copies, waits for them, and re-layouts: 3.71 us -> none
    pallas_call x1 -> x2, Pallas kernels: 16 us -> 16 us  [the longest x1 15.2 us: body(): pl.pallas_call(functools.partial(kernel, shards, groups), out_shape=(pltp...]
where the time goes in v2:
time: 16.8 us; the launch traced here: 16.6 us
  Pallas kernels  16 us (95%)
  between operations  0.64 us (4%)
    pallas_call x1, Pallas kernels, body(): pl.pallas_call(functools.partial(kernel, shards, groups), out_shape=(pltp...  15.2 us
    pallas_call x1, Pallas kernels, body(): pl.pallas_call(functools.partial(update, shards * groups * blocks * block...  0.79 us

profile of v2, /device:TPU:0, one launch (start us, length us, event | category | flops | bytes accessed | tf_op | source)
XLA Modules:
  0.0 16.6 jit_solution(14969773953350682283)
XLA Ops:
  0.6 15.2 %shard_map.119 = (f32[4,16,128]{2,1,0:T(8,128)S(1)}, f32[1,128]{1,0:T(1,128)S(1)}) custom-call(f32[16,128]{1,0:T(8,128)} %bitcast.12, bf16[16,128]{1,0:T(8,128)(2,1)} %bitcast.13, f32[1,16]{1,0:T(1,128)} %bitcast.15, bf16[16,128]{1,0:T(8,128)(2,1)} %bitcast.14, f32[1,16]{1,0:T(1,128)} %bitcast.16, bf16[8,16,128]{2,1,0:T(8,128)(2,1)} %bitcast.11, ...), custom_call_target="tpu_custom_call" | custom-call | tf_op jit(solution)/shard_map/pallas_call | solution.py:187
  15.8 0.8 %shard_map.120 = (f32[16,128]{1,0:T(8,128)}, bf16[16,128]{1,0:T(8,128)(2,1)}, f32[1,16]{1,0:T(1,128)}, bf16[16,128]{1,0:T(8,128)(2,1)}, f32[1,16]{1,0:T(1,128)}) custom-call(f32[4,16,128]{2,1,0:T(8,128)S(1)} %get-tuple-element.12.state, f32[1,128]{1,0:T(1,128)S(1)} %get-tuple-element.13.lanes), custom_call_target="tpu_custom_call" | custom-call | tf_op jit(solution)/shard_map/pallas_call | solution.py:220

commit v3 on v2

--- a/solution.py
+++ b/solution.py
@@ -36,14 +36,18 @@
     state_out, lanes_out,
     master_v, mc_v, vc_v, grads_v, m_wide, v_wide,
     ms_s, vs_s, order_s, place_s,
-    relay_out, relay_in, grad_in, square_out, square_in,
-    in_sems, grad_sems, relay_sems, square_sems,
+    relay_out, relay_in, grad_in, far_out, far_in, square_out, square_in, square_all,
+    in_sems, grad_sems, relay_sems, far_sems, square_sems,
 ):
     d = lax.axis_index("dp")
     e = lax.axis_index("expert")
     blocks, block = master_v.shape
     q = blocks // groups
-    total = shards * groups
+    half = shards // 2
+    summers = half * groups
+    me = d * groups + e
+    lower = d < half
+    upper = d >= half
 
     barrier = pltpu.get_barrier_semaphore()
 
@@ -53,8 +57,11 @@
     def greet_group(k):
         pl.semaphore_signal(barrier, inc=1, device_id=(d, lax.rem(e + k, groups)), device_id_type=MESH)
 
-    each(1, shards, greet_shard)
     each(1, groups, greet_group)
+
+    @pl.when(lower)
+    def _():
+        each(1, shards, greet_shard)
 
     loads = [
         pltpu.make_async_copy(src, dst, in_sems.at[i])
@@ -66,16 +73,32 @@
     for load in loads:
         load.start()
     loads[0].wait()
-    pl.semaphore_wait(barrier, shards - 1 + groups - 1)
-
-    def grad_copy(k):
-        to = lax.rem(d + k, shards)
-        return pltpu.make_async_remote_copy(
-            src_ref=grads_v.at[to], dst_ref=grad_in.at[k - 1],
+
+    @pl.when(lower)
+    def _():
+        pl.semaphore_wait(barrier, half - 1 + groups - 1)
+
+    @pl.when(upper)
+    def _():
+        pl.semaphore_wait(barrier, half + groups - 1)
+
+    def grad_copy(p):
+        return pltpu.make_async_remote_copy(
+            src_ref=grads_v.at[:, p], dst_ref=grad_in.at[d],
             send_sem=grad_sems.at[0], recv_sem=grad_sems.at[1],
-            device_id=(to, e), device_id_type=MESH)
-
-    each(1, shards, lambda k: grad_copy(k).start())
+            device_id=(p, e), device_id_type=MESH)
+
+    def send_grad(p):
+        @pl.when(d != p)
+        def _():
+            grad_copy(p).start()
+
+    each(0, half, send_grad)
+
+    @pl.when(lower)
+    def _():
+        for i in range(2):
+            grad_in[d, i] = grads_v[i, d]
 
     for load in loads[1:]:
         load.wait()
@@ -99,32 +122,48 @@
         if k:
             relay_copy(k).start()
 
-    whole = pltpu.make_async_remote_copy(
-        src_ref=grad_in, dst_ref=grad_in, send_sem=grad_sems.at[0], recv_sem=grad_sems.at[1],
-        device_id=(lax.rem(d + 1, shards), e), device_id_type=MESH)
-    whole.wait_recv()
-    gradient = grads_v[d].astype(jnp.float32)
-    if shards - 1 <= UNROLL:
-        for k in range(shards - 1):
-            gradient = gradient + grad_in[k].astype(jnp.float32)
-    else:
-        gradient = lax.fori_loop(
-            0, shards - 1, lambda k, g: g + grad_in[k].astype(jnp.float32), gradient)
-    squares = jnp.sum(gradient * gradient, axis=0, keepdims=True)
-    square_out[...] = squares
-
-    def square_copy(k):
-        flat = lax.rem(d * groups + e + k, total)
-        return pltpu.make_async_remote_copy(
-            src_ref=square_out, dst_ref=square_in.at[k - 1],
+    def some(ref, count, sems):
+        part = ref.at[pl.ds(0, count)]
+        return pltpu.make_async_remote_copy(
+            src_ref=part, dst_ref=part, send_sem=sems.at[0], recv_sem=sems.at[1],
+            device_id=(d, lax.rem(e + 1, groups)), device_id_type=MESH)
+
+    def far_copy():
+        return pltpu.make_async_remote_copy(
+            src_ref=far_out, dst_ref=far_in, send_sem=far_sems.at[0], recv_sem=far_sems.at[1],
+            device_id=(lax.rem(d + half, shards), e), device_id_type=MESH)
+
+    def square_copy(t):
+        return pltpu.make_async_remote_copy(
+            src_ref=square_out, dst_ref=square_in.at[me],
             send_sem=square_sems.at[0], recv_sem=square_sems.at[1],
-            device_id=(flat // groups, lax.rem(flat, groups)), device_id_type=MESH)
-
-    each(1, total, lambda k: square_copy(k).start())
-
-    relay_whole = pltpu.make_async_remote_copy(
-        src_ref=relay_in, dst_ref=relay_in, send_sem=relay_sems.at[0], recv_sem=relay_sems.at[1],
-        device_id=(d, lax.rem(e + 1, groups)), device_id_type=MESH)
+            device_id=(t // groups, t % groups), device_id_type=MESH)
+
+    def send_square(t):
+        @pl.when(me != t)
+        def _():
+            square_copy(t).start()
+
+    @pl.when(lower)
+    def _():
+        some(grad_in, shards - 1, grad_sems).wait_recv()
+        if shards <= UNROLL:
+            gradient = grad_in[0].astype(jnp.float32)
+            for k in range(1, shards):
+                gradient = gradient + grad_in[k].astype(jnp.float32)
+        else:
+            gradient = lax.fori_loop(
+                0, shards, lambda k, g: g + grad_in[k].astype(jnp.float32),
+                jnp.zeros((2, blocks, block), jnp.float32))
+        squares = jnp.sum(gradient[0] * gradient[0] + gradient[1] * gradient[1], axis=0, keepdims=True)
+        square_out[...] = squares
+        square_in[me] = squares
+        far_out[...] = gradient[1]
+        state_out[0] = gradient[0]
+        each(0, shards * groups, send_square)
+        far_copy().start()
+
+    relay_whole = some(relay_in, groups - 1, relay_sems)
     relay_whole.wait_recv()
     rows = lax.broadcasted_iota(jnp.int32, (blocks, block), 0)
     placed = [jnp.zeros((blocks, block), jnp.float32) for _ in range(3)]
@@ -135,21 +174,32 @@
             for i in range(3):
                 row = relay_out[0, i, c : c + 1, :] if k == 0 else relay_in[k - 1, i, c : c + 1, :]
                 placed[i] = jnp.where(here, jnp.broadcast_to(row, (blocks, block)), placed[i])
-    master, moment_one, moment_two = placed
-
     for i in range(3):
         state_out[i + 1] = placed[i]
-    state_out[0] = gradient
-
-    square_whole = pltpu.make_async_remote_copy(
-        src_ref=square_in, dst_ref=square_in, send_sem=square_sems.at[0], recv_sem=square_sems.at[1],
-        device_id=(lax.rem(d + 1, shards), e), device_id_type=MESH)
-    square_whole.wait_recv()
-    lanes_out[...] = jnp.sum(square_in[...], axis=0) + squares
-
-    whole.wait_send()
+
+    @pl.when(lower)
+    def _():
+        some(square_in, summers - 1, square_sems).wait_recv()
+
+    @pl.when(upper)
+    def _():
+        far_copy().wait_recv()
+        state_out[0] = far_in[...]
+        some(square_in, summers, square_sems).wait_recv()
+
+    lanes_out[...] = jnp.sum(square_in[...], axis=0)
+
     relay_whole.wait_send()
-    square_whole.wait_send()
+
+    @pl.when(lower)
+    def _():
+        some(grad_in, half - 1, grad_sems).wait_send()
+        far_copy().wait_send()
+        some(square_all, shards * groups - 1, square_sems).wait_send()
+
+    @pl.when(upper)
+    def _():
+        some(grad_in, half, grad_sems).wait_send()
 
 
 def update(count, state, lanes, master_out, mc_out, ms_out, vc_out, vs_out):
@@ -193,7 +243,7 @@
             pltpu.VMEM(wide, f32),
             pltpu.VMEM(wide, bf16),
             pltpu.VMEM(wide, bf16),
-            pltpu.VMEM((shards, blocks, block), bf16),
+            pltpu.VMEM((2, shards // 2, blocks, block), bf16),
             pltpu.VMEM(wide, f32),
             pltpu.VMEM(wide, f32),
             pltpu.SMEM((1, blocks), f32),
@@ -202,10 +252,14 @@
             pltpu.SMEM((1, blocks), jnp.int32),
             pltpu.VMEM((groups, 3, q, block), f32),
             pltpu.VMEM((groups - 1, 3, q, block), f32),
-            pltpu.VMEM((shards - 1, blocks, block), bf16),
+            pltpu.VMEM((shards, 2, blocks, block), bf16),
+            pltpu.VMEM(wide, f32),
+            pltpu.VMEM(wide, f32),
             pltpu.VMEM((1, block), f32),
+            pltpu.VMEM((shards // 2 * groups, 1, block), f32),
             pltpu.VMEM((shards * groups - 1, 1, block), f32),
             pltpu.SemaphoreType.DMA((8,)),
+            pltpu.SemaphoreType.DMA((2,)),
             pltpu.SemaphoreType.DMA((2,)),
             pltpu.SemaphoreType.DMA((2,)),
             pltpu.SemaphoreType.DMA((2,)),
@@ -214,7 +268,7 @@
     )(
         master_old.reshape(wide), m_codes.reshape(wide), m_scale.reshape(1, blocks),
         v_codes.reshape(wide), v_scale.reshape(1, blocks),
-        grad_parts.reshape(shards, blocks, block),
+        grad_parts.reshape(2, shards // 2, blocks, block),
         send_order.reshape(1, blocks), recv_place.reshape(1, blocks),
     )
     master_new, mc, ms, vc, vs = pl.pallas_call(

time: 16.8 us -> 14 us (0.83)
  Pallas kernels: 16 us -> 13.2 us
    pallas_call x1, Pallas kernels: 15.2 us -> 12.4 us  [body(): pl.pallas_call(functools.partial(kernel, shards, groups), out_shape=(pltp...]
where the time goes in v3:
time: 14 us; the launch traced here: 13.8 us
  Pallas kernels  13.2 us (94%)
  between operations  0.64 us (5%)
    pallas_call x1, Pallas kernels, body(): pl.pallas_call(functools.partial(kernel, shards, groups), out_shape=(pltp...  12.4 us
    pallas_call x1, Pallas kernels, body(): pl.pallas_call(functools.partial(update, shards * groups * blocks * block...  0.79 us

profile of v3, /device:TPU:0, one launch (start us, length us, event | category | flops | bytes accessed | tf_op | source)
XLA Modules:
  0.0 13.8 jit_solution(18003648244806947998)
XLA Ops:
  0.6 12.4 %shard_map.119 = (f32[4,16,128]{2,1,0:T(8,128)S(1)}, f32[1,128]{1,0:T(1,128)S(1)}) custom-call(f32[16,128]{1,0:T(8,128)} %bitcast.12, bf16[16,128]{1,0:T(8,128)(2,1)} %bitcast.13, f32[1,16]{1,0:T(1,128)} %bitcast.15, bf16[16,128]{1,0:T(8,128)(2,1)} %bitcast.14, f32[1,16]{1,0:T(1,128)} %bitcast.16, bf16[2,4,16,128]{3,2,1,0:T(8,128)(2,1)} %bitcast.11, ...), custom_call_target="tpu_custom_call" | custom-call | tf_op jit(solution)/shard_map/pallas_call | solution.py:237
  13.0 0.8 %shard_map.120 = (f32[16,128]{1,0:T(8,128)}, bf16[16,128]{1,0:T(8,128)(2,1)}, f32[1,16]{1,0:T(1,128)}, bf16[16,128]{1,0:T(8,128)(2,1)}, f32[1,16]{1,0:T(1,128)}) custom-call(f32[4,16,128]{2,1,0:T(8,128)S(1)} %get-tuple-element.12.state, f32[1,128]{1,0:T(1,128)S(1)} %get-tuple-element.13.lanes), custom_call_target="tpu_custom_call" | custom-call | tf_op jit(solution)/shard_map/pallas_call | solution.py:274

commit v4 on v3

--- a/solution.py
+++ b/solution.py
@@ -20,6 +20,7 @@
 
 MESH = pl.DeviceIdType.MESH
 UNROLL = 40
+SECTIONS = 8
 
 
 def each(first, last, step):
@@ -34,7 +35,7 @@
     shards, groups,
     master_in, mc_in, ms_in, vc_in, vs_in, grads_in, order_in, place_in,
     state_out, lanes_out,
-    master_v, mc_v, vc_v, grads_v, m_wide, v_wide,
+    master_v, mc_v, vc_v, m_wide, v_wide,
     ms_s, vs_s, order_s, place_s,
     relay_out, relay_in, grad_in, far_out, far_in, square_out, square_in, square_all,
     in_sems, grad_sems, relay_sems, far_sems, square_sems,
@@ -43,11 +44,11 @@
     e = lax.axis_index("expert")
     blocks, block = master_v.shape
     q = blocks // groups
-    half = shards // 2
-    summers = half * groups
+    part = shards // SECTIONS
+    summers = part * groups
     me = d * groups + e
-    lower = d < half
-    upper = d >= half
+    lower = d < part
+    upper = d >= part
 
     barrier = pltpu.get_barrier_semaphore()
 
@@ -66,25 +67,24 @@
     loads = [
         pltpu.make_async_copy(src, dst, in_sems.at[i])
         for i, (src, dst) in enumerate((
-            (grads_in, grads_v), (order_in, order_s), (ms_in, ms_s), (vs_in, vs_s),
+            (order_in, order_s), (ms_in, ms_s), (vs_in, vs_s),
             (mc_in, mc_v), (vc_in, vc_v), (master_in, master_v), (place_in, place_s),
         ))
     ]
     for load in loads:
         load.start()
-    loads[0].wait()
-
-    @pl.when(lower)
-    def _():
-        pl.semaphore_wait(barrier, half - 1 + groups - 1)
+
+    @pl.when(lower)
+    def _():
+        pl.semaphore_wait(barrier, part - 1 + groups - 1)
 
     @pl.when(upper)
     def _():
-        pl.semaphore_wait(barrier, half + groups - 1)
+        pl.semaphore_wait(barrier, part + groups - 1)
 
     def grad_copy(p):
         return pltpu.make_async_remote_copy(
-            src_ref=grads_v.at[:, p], dst_ref=grad_in.at[d],
+            src_ref=grads_in.at[:, p], dst_ref=grad_in.at[d],
             send_sem=grad_sems.at[0], recv_sem=grad_sems.at[1],
             device_id=(p, e), device_id_type=MESH)
 
@@ -93,14 +93,16 @@
         def _():
             grad_copy(p).start()
 
-    each(0, half, send_grad)
-
-    @pl.when(lower)
-    def _():
-        for i in range(2):
-            grad_in[d, i] = grads_v[i, d]
-
-    for load in loads[1:]:
+    each(0, part, send_grad)
+
+    def own_grad():
+        return pltpu.make_async_copy(grads_in.at[:, d], grad_in.at[d], in_sems.at[7])
+
+    @pl.when(lower)
+    def _():
+        own_grad().start()
+
+    for load in loads:
         load.wait()
     m_wide[...] = mc_v[...].astype(jnp.float32)
     v_wide[...] = vc_v[...].astype(jnp.float32)
@@ -128,10 +130,11 @@
             src_ref=part, dst_ref=part, send_sem=sems.at[0], recv_sem=sems.at[1],
             device_id=(d, lax.rem(e + 1, groups)), device_id_type=MESH)
 
-    def far_copy():
-        return pltpu.make_async_remote_copy(
-            src_ref=far_out, dst_ref=far_in, send_sem=far_sems.at[0], recv_sem=far_sems.at[1],
-            device_id=(lax.rem(d + half, shards), e), device_id_type=MESH)
+    def far_copy(i):
+        return pltpu.make_async_remote_copy(
+            src_ref=far_out.at[i - 1], dst_ref=far_in.at[0],
+            send_sem=far_sems.at[0], recv_sem=far_sems.at[1],
+            device_id=(lax.rem(d + i * part, shards), e), device_id_type=MESH)
 
     def square_copy(t):
         return pltpu.make_async_remote_copy(
@@ -146,6 +149,7 @@
 
     @pl.when(lower)
     def _():
+        own_grad().wait()
         some(grad_in, shards - 1, grad_sems).wait_recv()
         if shards <= UNROLL:
             gradient = grad_in[0].astype(jnp.float32)
@@ -154,14 +158,15 @@
         else:
             gradient = lax.fori_loop(
                 0, shards, lambda k, g: g + grad_in[k].astype(jnp.float32),
-                jnp.zeros((2, blocks, block), jnp.float32))
-        squares = jnp.sum(gradient[0] * gradient[0] + gradient[1] * gradient[1], axis=0, keepdims=True)
+                jnp.zeros((SECTIONS, blocks, block), jnp.float32))
+        squares = jnp.sum(jnp.sum(gradient * gradient, axis=0), axis=0, keepdims=True)
         square_out[...] = squares
         square_in[me] = squares
-        far_out[...] = gradient[1]
+        far_out[...] = gradient[1:]
         state_out[0] = gradient[0]
         each(0, shards * groups, send_square)
-        far_copy().start()
+        for i in range(1, SECTIONS):
+            far_copy(i).start()
 
     relay_whole = some(relay_in, groups - 1, relay_sems)
     relay_whole.wait_recv()
@@ -183,8 +188,8 @@
 
     @pl.when(upper)
     def _():
-        far_copy().wait_recv()
-        state_out[0] = far_in[...]
+        far_copy(1).wait_recv()
+        state_out[0] = far_in[0]
         some(square_in, summers, square_sems).wait_recv()
 
     lanes_out[...] = jnp.sum(square_in[...], axis=0)
@@ -193,13 +198,13 @@
 
     @pl.when(lower)
     def _():
-        some(grad_in, half - 1, grad_sems).wait_send()
-        far_copy().wait_send()
+        some(grad_in, part - 1, grad_sems).wait_send()
+        some(far_out, SECTIONS - 1, far_sems).wait_send()
         some(square_all, shards * groups - 1, square_sems).wait_send()
 
     @pl.when(upper)
     def _():
-        some(grad_in, half, grad_sems).wait_send()
+        some(grad_in, part, grad_sems).wait_send()
 
 
 def update(count, state, lanes, master_out, mc_out, ms_out, vc_out, vs_out):
@@ -243,7 +248,6 @@
             pltpu.VMEM(wide, f32),
             pltpu.VMEM(wide, bf16),
             pltpu.VMEM(wide, bf16),
-            pltpu.VMEM((2, shards // 2, blocks, block), bf16),
             pltpu.VMEM(wide, f32),
             pltpu.VMEM(wide, f32),
             pltpu.SMEM((1, blocks), f32),
@@ -252,11 +256,11 @@
             pltpu.SMEM((1, blocks), jnp.int32),
             pltpu.VMEM((groups, 3, q, block), f32),
             pltpu.VMEM((groups - 1, 3, q, block), f32),
-            pltpu.VMEM((shards, 2, blocks, block), bf16),
-            pltpu.VMEM(wide, f32),
-            pltpu.VMEM(wide, f32),
+            pltpu.VMEM((shards, SECTIONS, blocks, block), bf16),
+            pltpu.VMEM((SECTIONS - 1, blocks, block), f32),
+            pltpu.VMEM((1, blocks, block), f32),
             pltpu.VMEM((1, block), f32),
-            pltpu.VMEM((shards // 2 * groups, 1, block), f32),
+            pltpu.VMEM((shards // SECTIONS * groups, 1, block), f32),
             pltpu.VMEM((shards * groups - 1, 1, block), f32),
             pltpu.SemaphoreType.DMA((8,)),
             pltpu.SemaphoreType.DMA((2,)),
@@ -268,7 +272,7 @@
     )(
         master_old.reshape(wide), m_codes.reshape(wide), m_scale.reshape(1, blocks),
         v_codes.reshape(wide), v_scale.reshape(1, blocks),
-        grad_parts.reshape(2, shards // 2, blocks, block),
+        grad_parts.reshape(SECTIONS, shards // SECTIONS, blocks, block),
         send_order.reshape(1, blocks), recv_place.reshape(1, blocks),
     )
     master_new, mc, ms, vc, vs = pl.pallas_call(

time: 14 us -> 13.5 us (0.964)
  Pallas kernels: 13.2 us -> 12.7 us
    pallas_call x1, Pallas kernels: 12.4 us -> 11.9 us  [body(): pl.pallas_call(functools.partial(kernel, shards, groups), out_shape=(pltp...]
where the time goes in v4:
time: 13.5 us; the launch traced here: 13.3 us
  Pallas kernels  12.7 us (94%)
  between operations  0.64 us (5%)
    pallas_call x1, Pallas kernels, body(): pl.pallas_call(functools.partial(kernel, shards, groups), out_shape=(pltp...  11.9 us
    pallas_call x1, Pallas kernels, body(): pl.pallas_call(functools.partial(update, shards * groups * blocks * block...  0.79 us

profile of v4, /device:TPU:0, one launch (start us, length us, event | category | flops | bytes accessed | tf_op | source)
XLA Modules:
  0.0 13.3 jit_solution(10958698768133055512)
XLA Ops:
  0.6 11.9 %shard_map.119 = (f32[4,16,128]{2,1,0:T(8,128)S(1)}, f32[1,128]{1,0:T(1,128)S(1)}) custom-call(f32[16,128]{1,0:T(8,128)} %bitcast.12, bf16[16,128]{1,0:T(8,128)(2,1)} %bitcast.13, f32[1,16]{1,0:T(1,128)} %bitcast.15, bf16[16,128]{1,0:T(8,128)(2,1)} %bitcast.14, f32[1,16]{1,0:T(1,128)} %bitcast.16, bf16[8,1,16,128]{3,2,1,0:T(8,128)(2,1)} %bitcast.11, ...), custom_call_target="tpu_custom_call" | custom-call | tf_op jit(solution)/shard_map/pallas_call | solution.py:242
  12.5 0.8 %shard_map.120 = (f32[16,128]{1,0:T(8,128)}, bf16[16,128]{1,0:T(8,128)(2,1)}, f32[1,16]{1,0:T(1,128)}, bf16[16,128]{1,0:T(8,128)(2,1)}, f32[1,16]{1,0:T(1,128)}) custom-call(f32[4,16,128]{2,1,0:T(8,128)S(1)} %get-tuple-element.12.state, f32[1,128]{1,0:T(1,128)S(1)} %get-tuple-element.13.lanes), custom_call_target="tpu_custom_call" | custom-call | tf_op jit(solution)/shard_map/pallas_call | solution.py:278
